TPU v7x, 256 devices: a whole 4x4x8 slice. The times are simulated.
256 devices in a mesh: frame: 16 (over z_hi, y), space: 16 (over z_lo, x, core).
Axes of the slice: x: 4, y: 4, z: 8 (z_hi: 4, z_lo: 2; z = z_hi * 2 + z_lo), core: 2. Of those that a mesh axis runs over, the one named last changes fastest.
Arguments:
- hidden_in: bfloat16 [2, 16, 32, 64, 1152], P(None, 'frame', 'space'), may hold values from -6 to 6
- attn_cotangent: bfloat16 [2, 16, 32, 64, 1152], P(None, 'frame', 'space'), may hold values from -6 to 6
- w_qkv: bfloat16 [1152, 3456], P('space'), may hold values from -0.1875 to 0.1875
- modulation_table: bfloat16 [1000, 2, 1152], replicated, may hold values from -3 to 3
- snr_table: float32 [1000], replicated, may hold values from 0.1 to 1
- timestep: int32 [2], replicated, may hold values from 0 to 999
- weight_index: int32 [2], replicated, may hold values from 0 to 999
Outputs:
- grad_input: bfloat16 [2, 16, 32, 64, 1152], P(None, 'frame', 'space')
- grad_w_qkv: float32 [1152, 3456], P('space')
- grad_modulation: float32 [2, 2, 1152], replicated
All inputs are finite; a program needn't handle non-finite values.
Results may differ from a plain program's by a relative error of at most 0.029.
Values may be sent and summed in bfloat16 or wider, within the bound.
A program may use at most 128 MiB of HBM per device.

v0:
```python
import functools

import jax
import jax.numpy as jnp
from jax import lax
from jax.experimental import pallas as pl
from jax.experimental.pallas import tpu as pltpu
from jax.sharding import PartitionSpec as P

MESH = pl.DeviceIdType.MESH

HEADS = 16
HEAD_DIM = 72


def attend_back(queries, keys, values, upstream):
    factor = queries.shape[-1] ** (-0.5)
    f32 = jnp.float32
    high = lax.Precision.HIGH
    scores = jnp.einsum("bfxhe,bgxhe->bxhfg", queries, keys, preferred_element_type=f32) * factor
    expd = jnp.exp(scores)
    probs = expd / jnp.sum(expd, axis=-1, keepdims=True)
    grad_probs = jnp.einsum("bfxhe,bgxhe->bxhfg", upstream, values, preferred_element_type=f32)
    grad_values = jnp.einsum(
        "bxhfg,bfxhe->bgxhe", probs, upstream.astype(f32), precision=high
    )
    grad_scores = probs * (grad_probs - jnp.sum(probs * grad_probs, axis=-1, keepdims=True))
    grad_queries = jnp.einsum(
        "bxhfg,bgxhe->bfxhe", grad_scores, keys.astype(f32), precision=high
    ) * factor
    grad_keys = jnp.einsum(
        "bxhfg,bfxhe->bgxhe", grad_scores, queries.astype(f32), precision=high
    ) * factor
    return (
        grad_queries.astype(jnp.bfloat16),
        grad_keys.astype(jnp.bfloat16),
        grad_values.astype(jnp.bfloat16),
    )


def barrier_with(peers):
    barrier = pltpu.get_barrier_semaphore()
    for p in peers:
        pl.semaphore_signal(barrier, inc=1, device_id=p, device_id_type=MESH)
    pl.semaphore_wait(barrier, len(peers))


def exchange(src_ref, dst, peer_of, index_of, count, send_sem, recv_sem):
    sends = []
    for k in range(1, count):
        t = lax.rem(index_of + k, count)
        c = pltpu.make_async_remote_copy(
            src_ref=src_ref(t), dst_ref=dst.at[index_of], send_sem=send_sem.at[k],
            recv_sem=recv_sem.at[index_of], device_id=peer_of(t), device_id_type=MESH,
        )
        c.start()
        sends.append(c)
    return sends


def wait_all(src_ref, dst, peer_of, index_of, count, send_sem, recv_sem, sends):
    for k in range(1, count):
        src = lax.rem(index_of + count - k, count)
        pltpu.make_async_remote_copy(
            src_ref=src_ref(0), dst_ref=dst.at[src], send_sem=send_sem.at[k],
            recv_sem=recv_sem.at[src], device_id=peer_of(src), device_id_type=MESH,
        ).wait_recv()
    for c in sends:
        c.wait_send()


def space_parts(sub, s):
    nz, nx, nc = sub
    return (s // (nx * nc), lax.rem(s // nc, nx), lax.rem(s, nc))


def space_index(sub):
    nz, nx, nc = sub
    return (lax.axis_index("sz") * nx + lax.axis_index("sx")) * nc + lax.axis_index("sc")


def weight_kernel(nf, sub, chunks_ref, gw_ref, recv1, redbuf, recv2, s1, r1, s2, r2):
    me_f = lax.axis_index("frame")
    here = space_parts(sub, space_index(sub))
    peer = lambda t: (t,) + here
    barrier_with([peer(lax.rem(me_f + k, nf)) for k in range(1, nf)])
    first = lambda t: chunks_ref.at[t]
    sends = exchange(first, recv1, peer, me_f, nf, s1, r1)
    recv1[me_f] = chunks_ref[me_f]
    wait_all(first, recv1, peer, me_f, nf, s1, r1, sends)
    acc = recv1[0].astype(jnp.float32)
    for j in range(1, nf):
        acc = acc + recv1[j].astype(jnp.float32)
    acc = acc.astype(redbuf.dtype)
    redbuf[...] = acc
    recv2[me_f] = acc
    second = lambda t: redbuf
    sends = exchange(second, recv2, peer, me_f, nf, s2, r2)
    wait_all(second, recv2, peer, me_f, nf, s2, r2, sends)
    gw_ref[...] = recv2[...]


def sums_kernel(nf, sub, sums_ref, gm_ref, msum1, mbuf, msum2, s1, r1, s2, r2):
    ns = sub[0] * sub[1] * sub[2]
    me_f = lax.axis_index("frame")
    me_s = space_index(sub)
    fpeer = lambda t: (t,) + space_parts(sub, me_s)
    speer = lambda t: (me_f,) + space_parts(sub, t)
    barrier_with(
        [fpeer(lax.rem(me_f + k, nf)) for k in range(1, nf)]
        + [speer(lax.rem(me_s + k, ns)) for k in range(1, ns)]
    )
    first = lambda t: sums_ref
    sends = exchange(first, msum1, fpeer, me_f, nf, s1, r1)
    msum1[me_f] = sums_ref[...]
    wait_all(first, msum1, fpeer, me_f, nf, s1, r1, sends)
    macc = msum1[0]
    for j in range(1, nf):
        macc = macc + msum1[j]
    mbuf[...] = macc
    msum2[me_s] = macc
    second = lambda t: mbuf
    sends = exchange(second, msum2, speer, me_s, ns, s2, r2)
    wait_all(second, msum2, speer, me_s, ns, s2, r2, sends)
    total = msum2[0]
    for j in range(1, ns):
        total = total + msum2[j]
    gm_ref[...] = total


def reduce_weight(chunks, nf, sub):
    count, rows, cols = chunks.shape
    vmem = pl.BlockSpec(memory_space=pltpu.VMEM)
    return pl.pallas_call(
        functools.partial(weight_kernel, nf, sub),
        out_shape=jax.ShapeDtypeStruct((count, rows, cols), chunks.dtype),
        in_specs=[vmem],
        out_specs=vmem,
        scratch_shapes=[
            pltpu.VMEM((nf, rows, cols), chunks.dtype),
            pltpu.VMEM((rows, cols), chunks.dtype),
            pltpu.VMEM((nf, rows, cols), chunks.dtype),
        ]
        + [pltpu.SemaphoreType.DMA((nf,))] * 4,
        compiler_params=pltpu.CompilerParams(collective_id=0, has_side_effects=True),
    )(chunks)


def reduce_sums(sums, nf, sub):
    ns = sub[0] * sub[1] * sub[2]
    vmem = pl.BlockSpec(memory_space=pltpu.VMEM)
    return pl.pallas_call(
        functools.partial(sums_kernel, nf, sub),
        out_shape=jax.ShapeDtypeStruct(sums.shape, jnp.float32),
        in_specs=[vmem],
        out_specs=vmem,
        scratch_shapes=[
            pltpu.VMEM((nf,) + sums.shape, jnp.float32),
            pltpu.VMEM(sums.shape, jnp.float32),
            pltpu.VMEM((ns,) + sums.shape, jnp.float32),
        ]
        + [pltpu.SemaphoreType.DMA((nf,)), pltpu.SemaphoreType.DMA((nf,))]
        + [pltpu.SemaphoreType.DMA((ns,)), pltpu.SemaphoreType.DMA((ns,))],
        compiler_params=pltpu.CompilerParams(collective_id=1, has_side_effects=True),
    )(sums)


def per_device(
    hidden_in, attn_cotangent, w_qkv, modulation_table, snr_table, timestep, weight_index
):
    clip_count, frame_dev, row_dev, col_count, model_width = hidden_in.shape
    frame_n = lax.axis_size("frame")
    sub = (lax.axis_size("sz"), lax.axis_size("sx"), lax.axis_size("sc"))
    space_n = sub[0] * sub[1] * sub[2]
    positions = row_dev * col_count
    w_full = lax.all_gather(w_qkv, ("sz", "sx", "sc"), axis=0, tiled=True)
    both = jnp.stack(
        [
            hidden_in.reshape(clip_count, frame_dev, positions, model_width),
            attn_cotangent.reshape(clip_count, frame_dev, positions, model_width),
        ],
        axis=3,
    )
    both = lax.all_to_all(both, "frame", split_axis=2, concat_axis=1, tiled=True)
    frames = both.shape[1]
    across = both.shape[2]
    values_in = both[:, :, :, 0].astype(jnp.float32)
    average = jnp.mean(values_in, axis=-1, keepdims=True)
    centered = values_in - average
    variance = jnp.mean(centered * centered, axis=-1, keepdims=True)
    inverse_std = lax.rsqrt(variance + 1e-06)
    normed = centered * inverse_std
    modulation = modulation_table[timestep].astype(jnp.float32)
    shift = modulation[:, 0][:, None, None, :]
    scale = modulation[:, 1][:, None, None, :]
    modulated = (normed * (1.0 + scale) + shift).astype(jnp.bfloat16)
    mod_rows = modulated.reshape(-1, model_width)
    projected = jnp.dot(mod_rows, w_full, preferred_element_type=jnp.float32).astype(jnp.bfloat16)
    pieces = projected.reshape(clip_count, frames, across, 3, HEADS, HEAD_DIM)
    loss_weight = snr_table[weight_index]
    upstream = (
        loss_weight[:, None, None, None] * both[:, :, :, 1].astype(jnp.float32)
    ).astype(jnp.bfloat16)
    upstream = upstream.reshape(clip_count, frames, across, HEADS, HEAD_DIM)
    head_grads = attend_back(pieces[:, :, :, 0], pieces[:, :, :, 1], pieces[:, :, :, 2], upstream)
    grad_rows = jnp.stack(head_grads, axis=3).reshape(-1, 3 * model_width)
    grad_scale_factor = float(mod_rows.shape[0] * frame_n * space_n) ** (-0.5)
    term = lax.dot_general(
        mod_rows, grad_rows, (((0,), (0,)), ((), ())), preferred_element_type=jnp.float32
    ).astype(jnp.bfloat16)
    term, grad_rows = lax.optimization_barrier((term, grad_rows))
    col_blk = 3 * model_width // frame_n
    nz, nx, nc = sub
    row_blk = model_width // space_n
    share = term.reshape(nz, nx, nc, row_blk, 3 * model_width)
    share = lax.all_to_all(share, "sc", split_axis=2, concat_axis=2, tiled=True)
    share = jnp.sum(share.astype(jnp.float32), axis=2).astype(jnp.bfloat16)
    share = share.reshape(nz * nx, row_blk, 3 * model_width)
    share = lax.all_to_all(share, ("sz", "sx"), split_axis=0, concat_axis=0, tiled=True)
    share = jnp.sum(share.astype(jnp.float32), axis=0).astype(jnp.bfloat16)
    share = share.reshape(row_blk, frame_n, col_blk).transpose(1, 0, 2)
    grad_hidden = lax.dot_general(
        grad_rows, w_full, (((1,), (1,)), ((), ())), preferred_element_type=jnp.float32
    )
    grad_hidden = grad_hidden.reshape(values_in.shape)
    local_sums = jnp.stack(
        [jnp.sum(grad_hidden, axis=(1, 2)), jnp.sum(grad_hidden * normed, axis=(1, 2))],
        axis=1,
    )
    local_sums = local_sums.reshape(-1, model_width)
    gm = reduce_sums(local_sums, frame_n, sub)
    gw = reduce_weight(share, frame_n, sub).astype(jnp.float32)
    grad_weight = gw.transpose(1, 0, 2).reshape(row_blk, 3 * model_width) * grad_scale_factor
    grad_modulation = gm.reshape(clip_count, 2, model_width) * grad_scale_factor
    grad_normed = grad_hidden * (1.0 + scale)
    grad_input = (
        grad_normed
        - jnp.mean(grad_normed, axis=-1, keepdims=True)
        - normed * jnp.mean(grad_normed * normed, axis=-1, keepdims=True)
    ) * inverse_std
    grad_input = grad_input.astype(jnp.bfloat16)
    grad_input = lax.all_to_all(grad_input, "frame", split_axis=1, concat_axis=2, tiled=True)
    grad_input = grad_input.reshape(clip_count, frame_dev, row_dev, col_count, model_width)
    return (grad_input, grad_weight, grad_modulation)


def solution(mesh):
    space_sub = (2, 4, 2)
    devices = mesh.devices.reshape((mesh.shape["frame"],) + space_sub)
    fine = jax.sharding.Mesh(devices, ("frame", "sz", "sx", "sc"))
    space = ("sz", "sx", "sc")
    in_specs = (
        P(None, "frame", space, None, None),
        P(None, "frame", space, None, None),
        P(space, None),
        P(),
        P(),
        P(),
        P(),
    )
    out_specs = (P(None, "frame", space, None, None), P(space, None), P())
    return jax.shard_map(
        per_device, mesh=fine, in_specs=in_specs, out_specs=out_specs, check_vma=False
    )
```

profile of v0, /device:TPU:6, one launch (start us, length us, event | category | flops | bytes accessed | tf_op | source)
XLA Modules:
  0.0 299.9 jit_solution(15796300520601033023)
XLA Ops:
  11.3 2.7 pad_maximum_fusion.1
  13.9 11.2 %all-to-all-start = ((bf16[2,1,128,2,1152]{4,0,3,1,2:T(2,128)(2,1)}), bf16[2,1,128,2,1152]{4,0,3,1,2:T(2,128)(2,1)S(1)}, u32[]{:S(2)}, u32[]{:S(2)}) async-start(bf16[2,1,128,2,1152]{4,0,3,1,2:T(2,128)(2,1)} %pad_maximum_fusion.1), calls=%async_computation | async-start | bytes 2359296 | tf_op jit(solution)/shard_map/all_to_all | solution.py:184
  25.2 2.9 gather_fusion
  28.8 41.8 %all-to-all-done = bf16[2,1,128,2,1152]{4,0,3,1,2:T(2,128)(2,1)S(1)} async-done(((bf16[2,1,128,2,1152]{4,0,3,1,2:T(2,128)(2,1)}), bf16[2,1,128,2,1152]{4,0,3,1,2:T(2,128)(2,1)S(1)}, u32[]{:S(2)}, u32[]{:S(2)}) %all-to-all-start) | async-done | bytes 1179680 | tf_op jit(solution)/shard_map/all_to_all | solution.py:184
  72.6 2.9 reshape.191
  79.1 11.6 %all-gather.2.cloned.1.call-done = bf16[1152,3456]{1,0:T(8,128)(2,1)} async-done(((bf16[72,3456]{1,0:T(8,128)(2,1)}), bf16[1152,3456]{1,0:T(8,128)(2,1)}) %all-gather.2.cloned.1.call-update) | async-done | bytes 7962640 | tf_op jit(solution)/shard_map/all_gather | solution.py:176
  90.8 7.3 %convolution_convert_fusion.1 = bf16[256,3456]{1,0:T(8,128)(2,1)} fusion(bf16[256,1152]{1,0:T(8,128)(2,1)} %fusion.6, bf16[1152,3456]{1,0:T(8,128)(2,1)} %all-gather.2.cloned.1.call-done), kind=kOutput, calls=%fused_computation.3 | convolution fusion | flops 2039316480 | bytes 10321920 | tf_op jit(solution)/shard_map/dot_general | solution.py:198
  98.0 7.1 %reshape.182 = bf16[2,16,8,3,16,72]{5,4,3,2,1,0:T(8,128)(2,1)S(1)} reshape(bf16[256,3456]{1,0:T(8,128)(2,1)} %convolution_convert_fusion.1) | data formatting | bytes 3538944 | tf_op jit(solution)/shard_map/reshape | solution.py:199
  109.2 1.8 multiply_reduce_fusion
  112.7 1.9 fusion.3
  116.2 4.8 %reshape.183 = bf16[256,3456]{1,0:T(8,128)(2,1)} reshape(bf16[2,16,8,3,16,72]{5,4,3,2,1,0:T(8,128)(2,1)S(1)} %copy.71) | data formatting | bytes 3538944 | tf_op jit(solution)/shard_map/reshape | solution.py:206
  121.0 4.1 %convolution_convert_fusion = bf16[1152,3456]{1,0:T(8,128)(2,1)S(1)} fusion(bf16[256,1152]{1,0:T(8,128)(2,1)} %bitcast.109, bf16[256,3456]{1,0:T(8,128)(2,1)} %reshape.183), kind=kOutput, calls=%fused_computation.2 | convolution fusion | flops 2042413056 | bytes 10321920 | tf_op jit(solution)/shard_map/dot_general | solution.py:208
  125.2 7.0 %fusion.10 = (f32[256]{0:T(256)S(1)}, f32[256]{0:T(256)S(1)}, f32[256,1152]{1,0:T(8,128)}) fusion(f32[2,1152]{1,0:T(2,128)S(1)} %get-tuple-element.27, f32[256]{0:T(256)S(1)} %rsqrt.13, f32[256]{0:T(256)S(1)} %div.28, bf16[2,16,8,2,1152]{4,2,1,0,3:T(8,128)(2,1)S(1)} %bitcast.106, bf16[256,3456]{1,0:T(8,128)(2,1)S(1)} %copy-done.5, ...), kind=kOutput, calls=%fused_computation.36 | convolution fusion | flops 2040495616 | bytes 11514880 | tf_op jit(solution)/shard_map/dot_general | solution.py:222
  132.2 3.7 %copy.74 = bf16[2,4,2,72,3456]{4,3,1,0,2:T(8,128)(2,1)} copy(bf16[2,4,2,72,3456]{4,3,2,1,0:T(8,128)(2,1)S(1)} %bitcast.100) | data formatting | bytes 15925248 | tf_op jit(solution)/shard_map/reshape | solution.py:215
  135.9 6.9 %all-to-all-start.2 = ((bf16[2,4,2,72,3456]{4,3,1,0,2:T(8,128)(2,1)}), bf16[2,4,2,72,3456]{4,3,1,0,2:T(8,128)(2,1)}, u32[]{:S(2)}, u32[]{:S(2)}) async-start(bf16[2,4,2,72,3456]{4,3,1,0,2:T(8,128)(2,1)} %copy.74), calls=%async_computation.2 | async-start | bytes 15925248 | tf_op jit(solution)/shard_map/all_to_all | solution.py:216
  144.5 5.5 %all-to-all-done.2 = bf16[2,4,2,72,3456]{4,3,1,0,2:T(8,128)(2,1)} async-done(((bf16[2,4,2,72,3456]{4,3,1,0,2:T(8,128)(2,1)}), bf16[2,4,2,72,3456]{4,3,1,0,2:T(8,128)(2,1)}, u32[]{:S(2)}, u32[]{:S(2)}) %all-to-all-start.2) | async-done | bytes 7962656 | tf_op jit(solution)/shard_map/all_to_all | solution.py:216
  150.0 8.7 %all-to-all-start.1 = ((bf16[2,16,8,1152]{3,2,0,1:T(8,128)(2,1)}), bf16[2,16,8,1152]{3,2,0,1:T(8,128)(2,1)S(1)}, u32[]{:S(2)}, u32[]{:S(2)}) async-start(bf16[2,16,8,1152]{3,2,0,1:T(8,128)(2,1)} %copy.72), calls=%async_computation.1 | async-start | bytes 1179648 | tf_op jit(solution)/shard_map/all_to_all | solution.py:242
  158.7 7.8 %reduce_sum.102 = bf16[2,4,72,3456]{3,2,1,0:T(8,128)(2,1)} reduce(bf16[2,4,2,72,3456]{4,3,1,0,2:T(8,128)(2,1)} %all-to-all-done.2, bf16[]{:T(256)} %constant.23.clone.1), dimensions={2}, to_apply=%region_6.0 | reduce | flops 1990656 | bytes 11943938 | tf_op jit(solution)/shard_map/reduce_sum | solution.py:217
  166.5 9.1 %all-to-all-done.1 = bf16[2,16,8,1152]{3,2,0,1:T(8,128)(2,1)S(1)} async-done(((bf16[2,16,8,1152]{3,2,0,1:T(8,128)(2,1)}), bf16[2,16,8,1152]{3,2,0,1:T(8,128)(2,1)S(1)}, u32[]{:S(2)}, u32[]{:S(2)}) %all-to-all-start.1) | async-done | bytes 589856 | tf_op jit(solution)/shard_map/all_to_all | solution.py:242
  175.6 8.3 %all-to-all-start.3 = ((bf16[8,72,3456]{2,1,0:T(8,128)(2,1)}), bf16[8,72,3456]{2,1,0:T(8,128)(2,1)}, u32[]{:S(2)}, u32[]{:S(2)}) async-start(bf16[8,72,3456]{2,1,0:T(8,128)(2,1)} %bitcast.108), calls=%async_computation.3 | async-start | bytes 7962624 | tf_op jit(solution)/shard_map/all_to_all | solution.py:219
  184.6 56.0 %shard_map.95 = f32[4,1152]{1,0:T(4,128)} custom-call(f32[4,1152]{1,0:T(4,128)} %reshape.189.sums_ref), custom_call_target="tpu_custom_call" | custom-call | tf_op jit(solution)/shard_map/pallas_call | solution.py:152
  242.8 2.7 reduce_sum.103
  245.6 1.7 reshape.188
  248.3 41.5 %shard_map.94 = bf16[16,72,216]{2,1,0:T(8,128)(2,1)} custom-call(bf16[16,72,216]{2,1,0:T(8,128)(2,1)} %bitcast.110), custom_call_target="tpu_custom_call" | custom-call | tf_op jit(solution)/shard_map/pallas_call | solution.py:134
  (68 shorter events, 26.3 us)
Async XLA Ops:
  7.2 21.0 %copy-start = (f32[1000]{0:T(1024)S(1)}, f32[1000]{0:T(1024)}, u32[]{:S(2)}) copy-start(f32[1000]{0:T(1024)} %param.11) | copy-start | bytes 12004
  7.2 83.6 %all-gather.2.cloned.1.call-start = ((), (), s32[]{:S(2)}) async-start(), calls=%async_computation.4 | async-start | bytes 8460288 | tf_op jit(solution)/shard_map/all_gather | solution.py:176
  11.3 13.9 %copy-start.8 = (s32[2]{0:T(128)S(1)}, s32[2]{0:T(128)}, u32[]{:S(2)}) copy-start(s32[2]{0:T(128)} %param.12) | copy-start | bytes 28
  11.3 16.8 %copy-start.9 = (s32[2]{0:T(128)S(1)}, s32[2]{0:T(128)}, u32[]{:S(2)}) copy-start(s32[2]{0:T(128)} %param.13) | copy-start | bytes 28
  13.9 56.7 %all-to-all-start = ((bf16[2,1,128,2,1152]{4,0,3,1,2:T(2,128)(2,1)}), bf16[2,1,128,2,1152]{4,0,3,1,2:T(2,128)(2,1)S(1)}, u32[]{:S(2)}, u32[]{:S(2)}) async-start(bf16[2,1,128,2,1152]{4,0,3,1,2:T(2,128)(2,1)} %pad_maximum_fusion.1), calls=%async_computation | async-start | bytes 2359296 | tf_op jit(solution)/shard_map/all_to_all | solution.py:184
  70.8 7.2 %copy-start.2 = (bf16[2,1,128,2,1152]{4,2,0,3,1:T(8,128)(2,1)}, bf16[2,1,128,2,1152]{4,2,0,3,1:T(8,128)(2,1)S(1)}, u32[]{:S(2)}) copy-start(bf16[2,1,128,2,1152]{4,2,0,3,1:T(8,128)(2,1)S(1)} %copy.108) | copy-start | bytes 3538948
  105.8 1.7 copy-start.7
  121.0 4.2 %copy-start.3 = (bf16[2,1,128,2,1152]{4,2,0,3,1:T(8,128)(2,1)S(1)}, bf16[2,1,128,2,1152]{4,2,0,3,1:T(8,128)(2,1)}, u32[]{:S(2)}) copy-start(bf16[2,1,128,2,1152]{4,2,0,3,1:T(8,128)(2,1)} %copy-done.2) | copy-start | bytes 3538948
  121.0 4.2 %copy-start.5 = (bf16[256,3456]{1,0:T(8,128)(2,1)S(1)}, bf16[256,3456]{1,0:T(8,128)(2,1)}, u32[]{:S(2)}) copy-start(bf16[256,3456]{1,0:T(8,128)(2,1)} %reshape.183) | copy-start | bytes 5308420
  135.9 7.1 %copy-start.4 = (bf16[2,1,128,2,1152]{4,2,0,3,1:T(8,128)(2,1)S(1)}, bf16[2,1,128,2,1152]{4,2,0,3,1:T(8,128)(2,1)}, u32[]{:S(2)}) copy-start(bf16[2,1,128,2,1152]{4,2,0,3,1:T(8,128)(2,1)} %copy-done.2) | copy-start | bytes 3538948
  135.9 7.1 %copy-start.6 = (f32[256,1152]{1,0:T(8,128)S(1)}, f32[256,1152]{1,0:T(8,128)}, u32[]{:S(2)}) copy-start(f32[256,1152]{1,0:T(8,128)} %get-tuple-element.25) | copy-start | bytes 3538948
  135.9 14.1 %all-to-all-start.2 = ((bf16[2,4,2,72,3456]{4,3,1,0,2:T(8,128)(2,1)}), bf16[2,4,2,72,3456]{4,3,1,0,2:T(8,128)(2,1)}, u32[]{:S(2)}, u32[]{:S(2)}) async-start(bf16[2,4,2,72,3456]{4,3,1,0,2:T(8,128)(2,1)} %copy.74), calls=%async_computation.2 | async-start | bytes 15925248 | tf_op jit(solution)/shard_map/all_to_all | solution.py:216
  150.0 25.6 %all-to-all-start.1 = ((bf16[2,16,8,1152]{3,2,0,1:T(8,128)(2,1)}), bf16[2,16,8,1152]{3,2,0,1:T(8,128)(2,1)S(1)}, u32[]{:S(2)}, u32[]{:S(2)}) async-start(bf16[2,16,8,1152]{3,2,0,1:T(8,128)(2,1)} %copy.72), calls=%async_computation.1 | async-start | bytes 1179648 | tf_op jit(solution)/shard_map/all_to_all | solution.py:242
  175.6 67.2 %all-to-all-start.3 = ((bf16[8,72,3456]{2,1,0:T(8,128)(2,1)}), bf16[8,72,3456]{2,1,0:T(8,128)(2,1)}, u32[]{:S(2)}, u32[]{:S(2)}) async-start(bf16[8,72,3456]{2,1,0:T(8,128)(2,1)} %bitcast.108), calls=%async_computation.3 | async-start | bytes 7962624 | tf_op jit(solution)/shard_map/all_to_all | solution.py:219
  289.8 3.2 %copy-start.1 = (f32[1000]{0:T(1024)S(1)}, f32[1000]{0:T(1024)}, u32[]{:S(2)}) copy-start(f32[1000]{0:T(1024)} %param.11) | copy-start | bytes 12004
Sparse Core Ops, SparseCore 0:
  9.9 80.8 all-gather.1
where the time goes:
time: 301 us; the launch traced here: 300 us
  Pallas kernels  97.5 us (32%)
  waiting for transfers between devices  68.8 us (23%)
  local copies, waits for them, and re-layouts  35.2 us (12%)
  starting transfers between devices  35.1 us (12%)
  matrix products  27.1 us (9%)
  other arithmetic  21.7 us (7%)
  between operations  14.4 us (5%)
    pallas_call x1, Pallas kernels, reduce_sums(): pl.pallas_call(functools.partial(sums_kernel, nf, sub), out_shape=jax.Sha...  56 us
    all_to_all x1, waiting for transfers between devices, per_device(): lax.all_to_all(both, 'frame', split_axis=2, concat_axis=1, tiled=True)  41.8 us
    pallas_call x1, Pallas kernels, reduce_weight(): pl.pallas_call(functools.partial(weight_kernel, nf, sub), out_shape=jax.S...  41.5 us
    all_gather x1, waiting for transfers between devices, per_device(): w_full = lax.all_gather(w_qkv, ('sz', 'sx', 'sc'), axis=0, tiled=True)  11.6 us
    all_to_all x1, starting transfers between devices, per_device(): lax.all_to_all(both, 'frame', split_axis=2, concat_axis=1, tiled=True)  11.2 us
    all_to_all x1, waiting for transfers between devices, per_device(): lax.all_to_all(grad_input, 'frame', split_axis=1, concat_axis=2, tiled=True)  9.14 us
    all_to_all x1, starting transfers between devices, per_device(): lax.all_to_all(grad_input, 'frame', split_axis=1, concat_axis=2, tiled=True)  8.66 us
    all_to_all x1, starting transfers between devices, per_device(): lax.all_to_all(share, ('sz', 'sx'), split_axis=0, concat_axis=0, tiled=True)  8.29 us
  transfers between devices with their start and end apart: 5, of which 4 were waited for; matrix products, arithmetic and copies ran while one was open for 10% of the time, Pallas kernels for 19%

commit v1 on v0

--- a/solution.py
+++ b/solution.py
@@ -173,7 +173,10 @@
     sub = (lax.axis_size("sz"), lax.axis_size("sx"), lax.axis_size("sc"))
     space_n = sub[0] * sub[1] * sub[2]
     positions = row_dev * col_count
-    w_full = lax.all_gather(w_qkv, ("sz", "sx", "sc"), axis=0, tiled=True)
+    w_full = lax.all_gather(w_qkv, ("sz", "sx"), axis=0)
+    w_full = jnp.broadcast_to(w_full[:, None], (sub[0] * sub[1], sub[2]) + w_qkv.shape)
+    w_full = lax.all_to_all(w_full, "sc", split_axis=1, concat_axis=1, tiled=True)
+    w_full = w_full.reshape(-1, w_qkv.shape[1])
     both = jnp.stack(
         [
             hidden_in.reshape(clip_count, frame_dev, positions, model_width),
@@ -210,14 +213,8 @@
     ).astype(jnp.bfloat16)
     term, grad_rows = lax.optimization_barrier((term, grad_rows))
     col_blk = 3 * model_width // frame_n
-    nz, nx, nc = sub
-    row_blk = model_width // space_n
-    share = term.reshape(nz, nx, nc, row_blk, 3 * model_width)
-    share = lax.all_to_all(share, "sc", split_axis=2, concat_axis=2, tiled=True)
-    share = jnp.sum(share.astype(jnp.float32), axis=2).astype(jnp.bfloat16)
-    share = share.reshape(nz * nx, row_blk, 3 * model_width)
-    share = lax.all_to_all(share, ("sz", "sx"), split_axis=0, concat_axis=0, tiled=True)
-    share = jnp.sum(share.astype(jnp.float32), axis=0).astype(jnp.bfloat16)
+    share = lax.psum_scatter(term, ("sz", "sx", "sc"), scatter_dimension=0, tiled=True)
+    row_blk = share.shape[0]
     share = share.reshape(row_blk, frame_n, col_blk).transpose(1, 0, 2)
     grad_hidden = lax.dot_general(
         grad_rows, w_full, (((1,), (1,)), ((), ())), preferred_element_type=jnp.float32

time: 301 us -> 298 us (0.990)
  waiting for transfers between devices: 68.8 us -> 92.5 us
  Pallas kernels: 97.5 us -> 77.8 us
  starting transfers between devices: 35.1 us -> 20.8 us
  other arithmetic: 21.7 us -> 7.4 us
  blocking collectives: 0 us -> 11.4 us
  local copies, waits for them, and re-layouts: 35.2 us -> 44 us
    unnamed x1 -> x3, waiting for transfers between devices: 0.68 us -> 37.2 us
    pallas_call x1, Pallas kernels: 56 us -> 35.3 us  [reduce_sums(): pl.pallas_call(functools.partial(sums_kernel, nf, sub), out_shape=jax.Sha...]
    all_to_all x2 -> x0, starting transfers between devices: 15.2 us -> none  [the longest x1 8.29 us: per_device(): lax.all_to_all(share, ('sz', 'sx'), split_axis=0, concat_axis=0, tiled=True)]
    all_to_all x0 -> x1, blocking collectives: none -> 11.4 us  [per_device(): lax.all_to_all(w_full, 'sc', split_axis=1, concat_axis=1, tiled=True)]
    reduce_sum x3 -> x0, other arithmetic: 11.1 us -> none  [the longest x1 7.79 us: per_device(): share = jnp.sum(share.astype(jnp.float32), axis=2).astype(jnp.bfloat16)]
    all_to_all x1, waiting for transfers between devices: 9.14 us -> 0.01 us  [per_device(): lax.all_to_all(grad_input, 'frame', split_axis=1, concat_axis=2, tiled=True)]
    all_to_all x2 -> x0, waiting for transfers between devices: 5.5 us -> none  [the longest x1 5.5 us: per_device(): share = lax.all_to_all(share, 'sc', split_axis=2, concat_axis=2, tiled=True)]
    unnamed x23 -> x21, local copies, waits for them, and re-layouts: 3.42 us -> 8.3 us
  transfers between devices with their start and end apart: 5 -> 4, of which waited for: 4 -> 3; matrix products, arithmetic and copies ran while one was open for 10% -> 8% of each run, Pallas kernels for 19% -> 12%
where the time goes in v1:
time: 298 us; the launch traced here: 296 us
  waiting for transfers between devices  92.5 us (31%)
  Pallas kernels  77.8 us (26%)
  local copies, waits for them, and re-layouts  44 us (15%)
  matrix products  27.8 us (9%)
  starting transfers between devices  20.8 us (7%)
  between operations  14.4 us (5%)
  blocking collectives  11.4 us (4%)
  other arithmetic  7.4 us (2%)
    pallas_call x1, Pallas kernels, reduce_weight(): pl.pallas_call(functools.partial(weight_kernel, nf, sub), out_shape=jax.S...  42.5 us
    all_to_all x1, waiting for transfers between devices, per_device(): lax.all_to_all(both, 'frame', split_axis=2, concat_axis=1, tiled=True)  41.8 us
    unnamed x3, waiting for transfers between devices  37.2 us
    pallas_call x1, Pallas kernels, reduce_sums(): pl.pallas_call(functools.partial(sums_kernel, nf, sub), out_shape=jax.Sha...  35.3 us
    all_gather x1, waiting for transfers between devices, per_device(): w_full = lax.all_gather(w_qkv, ('sz', 'sx'), axis=0)  13.6 us
    all_to_all x1, blocking collectives, per_device(): lax.all_to_all(w_full, 'sc', split_axis=1, concat_axis=1, tiled=True)  11.4 us
    all_to_all x1, starting transfers between devices, per_device(): lax.all_to_all(both, 'frame', split_axis=2, concat_axis=1, tiled=True)  11.2 us
    all_to_all x1, starting transfers between devices, per_device(): lax.all_to_all(grad_input, 'frame', split_axis=1, concat_axis=2, tiled=True)  9.56 us
  transfers between devices with their start and end apart: 4, of which 3 were waited for; matrix products, arithmetic and copies ran while one was open for 8% of the time, Pallas kernels for 12%

profile of v1, /device:TPU:6, one launch (start us, length us, event | category | flops | bytes accessed | tf_op | source)
XLA Modules:
  0.0 296.2 jit_solution(17141825846283055262)
XLA Ops:
  11.3 2.6 pad_maximum_fusion.1
  13.9 11.2 %all-to-all-start = ((bf16[2,1,128,2,1152]{4,0,3,1,2:T(2,128)(2,1)}), bf16[2,1,128,2,1152]{4,0,3,1,2:T(2,128)(2,1)S(1)}, u32[]{:S(2)}, u32[]{:S(2)}) async-start(bf16[2,1,128,2,1152]{4,0,3,1,2:T(2,128)(2,1)} %pad_maximum_fusion.1), calls=%async_computation | async-start | bytes 2359296 | tf_op jit(solution)/shard_map/all_to_all | solution.py:187
  25.2 2.9 gather_fusion
  28.8 41.8 %all-to-all-done = bf16[2,1,128,2,1152]{4,0,3,1,2:T(2,128)(2,1)S(1)} async-done(((bf16[2,1,128,2,1152]{4,0,3,1,2:T(2,128)(2,1)}), bf16[2,1,128,2,1152]{4,0,3,1,2:T(2,128)(2,1)S(1)}, u32[]{:S(2)}, u32[]{:S(2)}) %all-to-all-start) | async-done | bytes 1179680 | tf_op jit(solution)/shard_map/all_to_all | solution.py:187
  70.8 3.1 %reshape.203 = f32[2,16,8,16,72]{4,3,2,1,0:T(8,128)} reshape(f32[2,16,8,1,1152]{4,2,1,0,3:T(8,128)S(1)} %slice_convert_fusion) | data formatting | bytes 2359296 | tf_op jit(solution)/shard_map/convert_element_type | solution.py:205
  75.5 13.6 %all-gather.3.cloned.1.call-done = bf16[576,3456]{1,0:T(8,128)(2,1)} async-done(((bf16[72,3456]{1,0:T(8,128)(2,1)}), bf16[576,3456]{1,0:T(8,128)(2,1)}) %all-gather.3.cloned.1.call-update) | async-done | bytes 3981328 | tf_op jit(solution)/shard_map/all_gather | solution.py:176
  89.1 2.7 broadcast_in_dim.7
  91.8 11.4 %all_to_all.26 = bf16[8,2,72,3456]{3,2,0,1:T(8,128)(2,1)} all-to-all(bf16[8,2,72,3456]{3,2,0,1:T(8,128)(2,1)S(1)} %broadcast_in_dim.7), channel_id=1, replica_groups=mesh['frame'=16,'sz'=2,'sx'=4,'sc'=2] {'sc'}, dimensions={1} | all-to-all | bytes 15925248 | tf_op jit(solution)/shard_map/all_to_all | solution.py:178
  103.2 3.8 %copy.41 = bf16[8,2,72,3456]{3,2,1,0:T(8,128)(2,1)S(1)} copy(bf16[8,2,72,3456]{3,2,0,1:T(8,128)(2,1)} %all_to_all.26) | data formatting | bytes 15925248 | tf_op jit(solution)/shard_map/all_to_all | solution.py:178
  107.0 3.1 %copy-done.4 = bf16[8,2,72,3456]{3,2,1,0:T(8,128)(2,1)} copy-done((bf16[8,2,72,3456]{3,2,1,0:T(8,128)(2,1)}, bf16[8,2,72,3456]{3,2,1,0:T(8,128)(2,1)S(1)}, u32[]{:S(2)}) %copy-start.4) | copy-done | bytes 7962648
  110.1 4.9 %convolution_convert_fusion.1 = bf16[256,3456]{1,0:T(8,128)(2,1)} fusion(bf16[256,1152]{1,0:T(8,128)(2,1)} %bitcast.109, bf16[1152,3456]{1,0:T(8,128)(2,1)S(1)} %bitcast.105), kind=kOutput, calls=%fused_computation.3 | convolution fusion | flops 2039316480 | bytes 10321920 | tf_op jit(solution)/shard_map/dot_general | solution.py:201
  114.9 7.1 %reshape.198 = bf16[2,16,8,3,16,72]{5,4,3,2,1,0:T(8,128)(2,1)S(1)} reshape(bf16[256,3456]{1,0:T(8,128)(2,1)} %convolution_convert_fusion.1) | data formatting | bytes 3538944 | tf_op jit(solution)/shard_map/reshape | solution.py:202
  124.7 2.3 multiply_reduce_fusion
  127.0 1.9 fusion.4
  128.9 1.7 fusion.5
  130.7 2.1 fusion.3
  134.6 4.6 %reshape.199 = bf16[256,3456]{1,0:T(8,128)(2,1)} reshape(bf16[2,16,8,3,16,72]{5,4,3,2,1,0:T(8,128)(2,1)S(1)} %copy.47) | data formatting | bytes 3538944 | tf_op jit(solution)/shard_map/reshape | solution.py:209
  139.2 7.2 %convolution_convert_fusion = bf16[1152,3456]{1,0:T(8,128)(2,1)} fusion(bf16[256,1152]{1,0:T(8,128)(2,1)} %bitcast.110, bf16[256,3456]{1,0:T(8,128)(2,1)} %reshape.199), kind=kOutput, calls=%fused_computation.2 | convolution fusion | flops 2042413056 | bytes 10321920 | tf_op jit(solution)/shard_map/dot_general | solution.py:211
  148.2 6.1 %fusion.19 = (f32[2,1152]{1,0:T(2,128)S(1)}, f32[2,16,8]{2,1,0:T(8,128)S(1)}, f32[2,16,8]{2,1,0:T(8,128)S(1)}, f32[2,1152]{1,0:T(2,128)S(1)}, f32[2,16,8,1152]{3,2,1,0:T(8,128)S(1)}) fusion(f32[2,16,8]{2,1,0:T(8,128)S(1)} %add_rsqrt_fusion, f32[2,16,8]{2,1,0:T(8,128)S(1)} %broadcast_multiply_fusion.3, bf16[2,16,8,2,1152]{4,2,1,0,3:T(8,128)(2,1)S(1)} %bitcast.103, ...), kind=kOutput, calls=%fused_computation.33 | convolution fusion | flops 2041375744 | bytes 11533312 | tf_op jit(solution)/shard_map/dot_general | solution.py:219
  155.6 9.6 %all-to-all-start.2 = ((bf16[2,16,8,1152]{3,2,0,1:T(8,128)(2,1)}), bf16[2,16,8,1152]{3,2,0,1:T(8,128)(2,1)S(1)}, u32[]{:S(2)}, u32[]{:S(2)}) async-start(bf16[2,16,8,1152]{3,2,0,1:T(8,128)(2,1)} %copy.48), calls=%async_computation.2 | async-start | bytes 1179648 | tf_op jit(solution)/shard_map/all_to_all | solution.py:239
  165.9 35.3 %shard_map.95 = f32[4,1152]{1,0:T(4,128)} custom-call(f32[4,1152]{1,0:T(4,128)} %reshape.202.sums_ref), custom_call_target="tpu_custom_call" | custom-call | tf_op jit(solution)/shard_map/pallas_call | solution.py:152
  203.4 36.5 %reduce-scatter.5.cloned.1.call-done = bf16[72,3456]{1,0:T(8,128)(2,1)} async-done(((bf16[1152,3456]{1,0:T(8,128)(2,1)}), bf16[72,3456]{1,0:T(8,128)(2,1)}) %reduce-scatter.5.cloned.1.call-update) | async-done | bytes 497680
  239.9 2.8 reshape.201
  243.7 42.5 %shard_map.94 = bf16[16,72,216]{2,1,0:T(8,128)(2,1)} custom-call(bf16[16,72,216]{2,1,0:T(8,128)(2,1)} %bitcast.111), custom_call_target="tpu_custom_call" | custom-call | tf_op jit(solution)/shard_map/pallas_call | solution.py:134
  (59 shorter events, 21.3 us)
Async XLA Ops:
  7.2 21.0 %copy-start = (f32[1000]{0:T(1024)S(1)}, f32[1000]{0:T(1024)}, u32[]{:S(2)}) copy-start(f32[1000]{0:T(1024)} %param.11) | copy-start | bytes 12004
  7.2 81.9 %all-gather.3.cloned.1.call-start = ((), (), s32[]{:S(2)}) async-start(), calls=%async_computation.4 | async-start | bytes 4478976 | tf_op jit(solution)/shard_map/all_gather | solution.py:176
  11.3 13.9 %copy-start.7 = (s32[2]{0:T(128)S(1)}, s32[2]{0:T(128)}, u32[]{:S(2)}) copy-start(s32[2]{0:T(128)} %param.12) | copy-start | bytes 28
  11.3 16.8 %copy-start.8 = (s32[2]{0:T(128)S(1)}, s32[2]{0:T(128)}, u32[]{:S(2)}) copy-start(s32[2]{0:T(128)} %param.13) | copy-start | bytes 28
  13.9 56.7 %all-to-all-start = ((bf16[2,1,128,2,1152]{4,0,3,1,2:T(2,128)(2,1)}), bf16[2,1,128,2,1152]{4,0,3,1,2:T(2,128)(2,1)S(1)}, u32[]{:S(2)}, u32[]{:S(2)}) async-start(bf16[2,1,128,2,1152]{4,0,3,1,2:T(2,128)(2,1)} %pad_maximum_fusion.1), calls=%async_computation | async-start | bytes 2359296 | tf_op jit(solution)/shard_map/all_to_all | solution.py:187
  25.1 214.8 %reduce-scatter.5.cloned.1.call-start = ((), (), s32[]{:S(2)}) async-start(), calls=%async_computation.5 | async-start | bytes 8460288
  70.7 3.7 %copy-start.2 = (bf16[2,1,128,2,1152]{4,2,0,3,1:T(8,128)(2,1)}, bf16[2,1,128,2,1152]{4,2,0,3,1:T(8,128)(2,1)S(1)}, u32[]{:S(2)}) copy-start(bf16[2,1,128,2,1152]{4,2,0,3,1:T(8,128)(2,1)S(1)} %copy.85) | copy-start | bytes 3538948
  107.0 3.1 %copy-start.4 = (bf16[8,2,72,3456]{3,2,1,0:T(8,128)(2,1)}, bf16[8,2,72,3456]{3,2,1,0:T(8,128)(2,1)S(1)}, u32[]{:S(2)}) copy-start(bf16[8,2,72,3456]{3,2,1,0:T(8,128)(2,1)S(1)} %copy.41) | copy-start | bytes 23887876
  123.0 1.7 copy-start.6
  146.4 1.3 copy-start.3
  146.4 1.8 copy-start.5
  155.6 46.9 %all-to-all-start.2 = ((bf16[2,16,8,1152]{3,2,0,1:T(8,128)(2,1)}), bf16[2,16,8,1152]{3,2,0,1:T(8,128)(2,1)S(1)}, u32[]{:S(2)}, u32[]{:S(2)}) async-start(bf16[2,16,8,1152]{3,2,0,1:T(8,128)(2,1)} %copy.48), calls=%async_computation.2 | async-start | bytes 1179648 | tf_op jit(solution)/shard_map/all_to_all | solution.py:239
  286.1 3.2 %copy-start.1 = (f32[1000]{0:T(1024)S(1)}, f32[1000]{0:T(1024)}, u32[]{:S(2)}) copy-start(f32[1000]{0:T(1024)} %param.11) | copy-start | bytes 12004
Sparse Core Ops, SparseCore 0:
  9.8 79.2 all-gather.2
  146.5 93.2 reduce-scatter.4
